TPU v7x, 256 devices: a whole 4x4x8 slice. The times are simulated.
256 devices in a mesh: dom: 64 (over z, x, core), bin: 4 (over y).
Axes of the slice: x: 4, y: 4, z: 8, core: 2. Of those that a mesh axis runs over, the one named last changes fastest.
Arguments:
- points: float32 [3, 524288], P(None, ('dom', 'bin')), may hold values from 0 to 8, as said below
- candidates: int32 [16, 524288], P(None, ('dom', 'bin')), may hold values from 0 to 127, as said below
- block_dom: int32 [4096], P(('dom', 'bin')), may hold values from 0 to 63, as said below
- block_bin: int32 [4096], P(('dom', 'bin')), may hold values from 0 to 3, as said below
- block_slot: int32 [4096], P(('dom', 'bin')), may hold values from 0 to 31
- donor_nodes: float32 [81, 1048576], P(None, ('dom', 'bin')), may hold values from -1 to 9
- donor_flow: float32 [135, 1048576], P(None, ('dom', 'bin')), may hold values from -6 to 6
Outputs:
- blended: float32 [5, 524288], P(None, ('dom', 'bin'))
Inputs may be any that keep to these rules, and one draw needn't show every extreme that they name: Cell c of a donor block sits at lattice position (c // 32, c // 8 % 4, c % 8) of a 4 x 4 x 8 brick of unit cells; the 16 candidates of a receptor are the cells of one 2 x 2 x 4 box of that brick, in a random order, and the receptor lies within that box. `points`: coordinates in the frame of the donor brick. `block_bin`: the 16 blocks of each device name every bin exactly 4 times. `block_dom`: take the blocks of the 4 devices that share one dom index and name one bin q: no dom index is named more than 2 times among them, and for every q the same 4 dom indices are named exactly 2 times by every such group.
All inputs are finite; a program needn't handle non-finite values.
Results may differ from a plain program's by a relative error of at most 0.0003.
Values sent between devices are 32-bit elements; how exact they have to be, the bound alone decides.
A program may use at most 128 MiB of HBM per device.

v0:
```python
import jax
import jax.numpy as jnp
from jax import lax
from jax.sharding import PartitionSpec as P

VARS = 5
CELLS_BLK = 128
STEPS = 6


clamp_edge = 1.25
relax_factor = 0.5
sharpness = 16.0
group_blocks = 8


def lagrange(coord):
    values = jnp.stack(
        [0.5 * coord * (coord - 1.0), 1.0 - coord * coord, 0.5 * coord * (coord + 1.0)]
    )
    slopes = jnp.stack([coord - 0.5, -2.0 * coord, coord + 0.5])
    return (values, slopes)


def tensor_basis(first, second, third):
    joined = first[:, None, None] * second[None, :, None] * third[None, None, :]
    return joined.reshape((27,) + first.shape[1:])


def shapes_at(ref_point):
    value_x, slope_x = lagrange(ref_point[0])
    value_y, slope_y = lagrange(ref_point[1])
    value_z, slope_z = lagrange(ref_point[2])
    return (
        tensor_basis(value_x, value_y, value_z),
        tensor_basis(slope_x, value_y, value_z),
        tensor_basis(value_x, slope_y, value_z),
        tensor_basis(value_x, value_y, slope_z),
    )


def cross_product(left, right):
    return jnp.stack(
        [
            left[1] * right[2] - left[2] * right[1],
            left[2] * right[0] - left[0] * right[2],
            left[0] * right[1] - left[1] * right[0],
        ]
    )


def blend_points(points, cells, flows):
    geometry = cells.reshape((3, 27) + cells.shape[1:])
    ref_point = jnp.zeros((3,) + cells.shape[1:], jnp.float32)
    for sweep in range(STEPS):
        weight_fn, along_x, along_y, along_z = shapes_at(ref_point)
        position = jnp.sum(geometry * weight_fn[None], axis=1)
        column_x = jnp.sum(geometry * along_x[None], axis=1)
        column_y = jnp.sum(geometry * along_y[None], axis=1)
        column_z = jnp.sum(geometry * along_z[None], axis=1)
        misfit = position - points[:, None, :]
        normal_yz = cross_product(column_y, column_z)
        determinant = jnp.sum(column_x * normal_yz, axis=0)
        step_x = jnp.sum(misfit * normal_yz, axis=0)
        step_y = jnp.sum(column_x * cross_product(misfit, column_z), axis=0)
        step_z = jnp.sum(column_x * cross_product(column_y, misfit), axis=0)
        update = jnp.stack([step_x, step_y, step_z]) / determinant[None]
        ref_point = jnp.clip(ref_point - relax_factor * update, -clamp_edge, clamp_edge)
    weight_fn = shapes_at(ref_point)[0]
    fields = jnp.sum(flows.reshape((VARS, 27) + flows.shape[1:]) * weight_fn[None], axis=1)
    excess = jnp.sum(jnp.square(jnp.maximum(jnp.abs(ref_point) - 1.0, 0.0)), axis=0)
    trust = 1.0 / (1.0 + sharpness * excess)
    return jnp.sum(fields * trust[None], axis=1) / jnp.sum(trust, axis=0)[None]


def blend_columns(points, cell_ids, nodes, flows, width):
    total = points.shape[1]
    span = group_blocks * width

    def advance(group, result):
        start = group * span
        chosen = lax.dynamic_slice_in_dim(points, start, span, 1)
        ids = lax.dynamic_slice_in_dim(cell_ids, start, span, 1)
        cells = jnp.take(nodes, ids, axis=1)
        values = jnp.take(flows, ids, axis=1)
        return lax.dynamic_update_slice_in_dim(
            result, blend_points(chosen, cells, values), start, 1
        )

    return lax.fori_loop(0, total // span, advance, jnp.zeros((VARS, total), jnp.float32))


def ranks_within(labels):
    count = labels.shape[0]
    order = jnp.arange(count, dtype=jnp.int32)
    earlier = (labels[None, :] == labels[:, None]) & (order[None, :] < order[:, None])
    return jnp.sum(earlier.astype(jnp.int32), axis=1)


def slot_sources(position, total):
    match = (jnp.arange(total, dtype=jnp.int32)[:, None] == position[None, :]).astype(jnp.int32)
    return jnp.sum(match * jnp.arange(position.shape[0], dtype=jnp.int32)[None, :], axis=1)


def local(points, candidates, block_dom, block_bin, block_slot, donor_nodes, donor_flow):
    bin_count = lax.axis_size("bin")
    dom_count = lax.axis_size("dom")
    blocks = block_dom.shape[0]
    per_bin = blocks // bin_count
    per_dom = max(2, 4 * blocks // dom_count)
    slots_all = dom_count * per_dom
    width = points.shape[1] // blocks
    send_pos = block_bin * per_bin + ranks_within(block_bin)
    send_src = slot_sources(send_pos, blocks)
    route = jnp.stack([block_dom, block_slot])[:, send_src].reshape(2, bin_count, per_bin)
    route = lax.all_to_all(route, "bin", split_axis=1, concat_axis=1, tiled=True).reshape(2, blocks)
    middle_pos = route[0] * per_dom + ranks_within(route[0])
    middle_src = slot_sources(middle_pos, slots_all)
    wanted = route[1][middle_src].reshape(dom_count, per_dom)
    wanted = lax.all_to_all(wanted, "dom", split_axis=0, concat_axis=0, tiled=True).reshape(
        slots_all
    )
    node_rows = donor_nodes.reshape(donor_nodes.shape[0], -1, CELLS_BLK)[:, wanted]
    flow_rows = donor_flow.reshape(donor_flow.shape[0], -1, CELLS_BLK)[:, wanted]
    node_rows = node_rows.reshape(-1, dom_count, per_dom, CELLS_BLK)
    flow_rows = flow_rows.reshape(-1, dom_count, per_dom, CELLS_BLK)
    node_rows, flow_rows = (
        lax.all_to_all(node_rows, "dom", split_axis=1, concat_axis=1, tiled=True),
        lax.all_to_all(flow_rows, "dom", split_axis=1, concat_axis=1, tiled=True),
    )
    node_rows = node_rows.reshape(-1, slots_all, CELLS_BLK)[:, middle_pos]
    flow_rows = flow_rows.reshape(-1, slots_all, CELLS_BLK)[:, middle_pos]
    node_rows = node_rows.reshape(-1, bin_count, per_bin, CELLS_BLK)
    flow_rows = flow_rows.reshape(-1, bin_count, per_bin, CELLS_BLK)
    node_rows, flow_rows = (
        lax.all_to_all(node_rows, "bin", split_axis=1, concat_axis=1, tiled=True),
        lax.all_to_all(flow_rows, "bin", split_axis=1, concat_axis=1, tiled=True),
    )
    node_rows = node_rows.reshape(-1, blocks * CELLS_BLK)
    flow_rows = flow_rows.reshape(-1, blocks * CELLS_BLK)
    offsets = jnp.repeat(send_pos * CELLS_BLK, width, total_repeat_length=blocks * width)
    cell_ids = candidates + offsets[None, :]
    return blend_columns(points, cell_ids, node_rows, flow_rows, width)


def solution(mesh):
    return jax.shard_map(
        local,
        mesh=mesh,
        in_specs=(
            P(None, ("dom", "bin")),
            P(None, ("dom", "bin")),
            P(("dom", "bin")),
            P(("dom", "bin")),
            P(("dom", "bin")),
            P(None, ("dom", "bin")),
            P(None, ("dom", "bin")),
        ),
        out_specs=P(None, ("dom", "bin")),
        check_vma=False,
    )
```

profile of v0, /device:TPU:1, one launch (start us, length us, event | category | flops | bytes accessed | tf_op | source)
XLA Modules:
  0.0 797.1 jit_solution(12911579697675497308)
XLA Ops:
  3.2 8.9 %all_to_all.34 = s32[2,4,4]{2,0,1:T(2,128)S(1)} all-to-all(s32[2,4,4]{2,0,1:T(2,128)S(1)} %copy.63), channel_id=1, replica_groups=mesh['dom'=64,'bin'=4] {'bin'}, dimensions={1} | all-to-all | bytes 256 | tf_op jit(solution)/shard_map/all_to_all | solution.py:116
  13.3 9.9 %bitcast_select_fusion.8 = s32[128]{0:T(128)S(1)} fusion(s32[128]{0:T(128)S(1)} %select_reduce_fusion, s32[]{:T(128)} %bitcast.97, s32[]{:T(128)} %bitcast.98, s32[]{:T(128)} %bitcast.99, s32[]{:T(128)} %bitcast.100, s32[]{:T(128)} %bitcast.101, s32[]{:T(128)} %bitcast.103, s32[]{:T(128)} %bitcast.102, s32[]{:T(128)} %bitcast.80, s32[]{:T(128)} %bitcast.82, ...), kind=kLoop, calls=%fused_computation.392 | loop fusion | flops 4224 | bytes 1088 | tf_op jit(solution)/shard_map/gather | solution.py:119
  24.0 13.6 %all-to-all-start.1 = ((s32[64,1,2]{2,1,0:T(1,128)}), s32[64,1,2]{2,1,0:T(1,128)S(1)}, u32[]{:S(2)}, u32[]{:S(2)}) async-start(s32[64,1,2]{2,1,0:T(1,128)} %bitcast.105), calls=%async_computation.1 | async-start | bytes 65536 | tf_op jit(solution)/shard_map/all_to_all | solution.py:120
  40.1 6.8 all-to-all-done.1
  51.7 7.8 copy.71
  59.5 5.7 all-to-all-start.4
  73.3 13.9 %copy.66 = f32[135,64,2,128]{3,2,0,1:T(2,128)} copy(f32[135,64,2,128]{3,0,2,1:T(8,128)} %bitcast.358) | data formatting | bytes 17694720 | tf_op jit(solution)/shard_map/reshape | solution.py:126
  87.2 96.1 %all-to-all-done.4 = f32[81,64,2,128]{3,2,0,1:T(2,128)} async-done(((f32[81,64,2,128]{3,2,0,1:T(2,128)}), f32[81,64,2,128]{3,2,0,1:T(2,128)}, u32[]{:S(2)}, u32[]{:S(2)}) %all-to-all-start.4) | async-done | bytes 5308448 | tf_op jit(solution)/shard_map/all_to_all | solution.py:128
  183.3 8.1 %all-to-all-start.2 = ((f32[135,64,2,128]{3,2,0,1:T(2,128)}), f32[135,64,2,128]{3,2,0,1:T(2,128)}, u32[]{:S(2)}, u32[]{:S(2)}) async-start(f32[135,64,2,128]{3,2,0,1:T(2,128)} %copy.66), calls=%async_computation.2 | async-start | bytes 17694720 | tf_op jit(solution)/shard_map/all_to_all | solution.py:129
  191.5 5.5 copy.72
  201.2 182.7 %all-to-all-done.2 = f32[135,64,2,128]{3,2,0,1:T(2,128)} async-done(((f32[135,64,2,128]{3,2,0,1:T(2,128)}), f32[135,64,2,128]{3,2,0,1:T(2,128)}, u32[]{:S(2)}, u32[]{:S(2)}) %all-to-all-start.2) | async-done | bytes 8847392 | tf_op jit(solution)/shard_map/all_to_all | solution.py:129
  388.1 7.7 copy.67
  410.1 5.6 select_select_fusion
  419.3 377.8 %while.17 = (s32[]{:T(128)}, f32[5,2048]{1,0:T(8,128)}, s32[16,2048]{1,0:T(8,128)}, f32[135,2048]{0,1:T(8,128)S(1)}, f32[81,2048]{0,1:T(8,128)S(1)}, /*index=5*/...) while((s32[]{:T(128)}, f32[5,2048]{1,0:T(8,128)}, ...), condition=%wide.region_57.58_spmd, body=%wide.region_4.57_spmd.sunk | while | flops 110738432 | bytes 286155008 | solution.py:90
  424.3 59.6 %gather_fusion.1 = f32[16384,81]{1,0:T(8,128)} fusion(f32[81,2048]{0,1:T(8,128)S(1)} %get-tuple-element.1132, s32[16384]{0:T(1024)} %broadcast_clamp_fusion.2), kind=kCustom, calls=%fused_computation.1.clone.1 | custom fusion | bytes 10682368 | tf_op jit(solution)/shard_map/while/body/eval_jaxpr/jit(_take)/gather | solution.py:84
  484.0 8.2 %copy.91 = f32[16,1024,81]{1,0,2:T(8,128)} copy(f32[16,1024,81]{2,1,0:T(8,128)} %bitcast.287) | data formatting | bytes 10616832 | tf_op jit(solution)/shard_map/while/body/eval_jaxpr/jit(_take)/gather | solution.py:84
  493.0 5.4 multiply_reduce_fusion.55
  520.0 66.9 %gather_fusion = f32[16384,135]{1,0:T(8,128)} fusion(f32[135,2048]{0,1:T(8,128)S(1)} %get-tuple-element.1131, s32[16384]{0:T(1024)} %broadcast_clamp_fusion.2), kind=kCustom, calls=%fused_computation.clone.1 | custom fusion | bytes 17760256 | tf_op jit(solution)/shard_map/while/body/eval_jaxpr/jit(_take)/gather | solution.py:85
  586.8 15.2 %copy.90 = f32[16,1024,135]{1,0,2:T(8,128)} copy(f32[16,1024,135]{2,1,0:T(8,128)} %bitcast.285) | data formatting | bytes 17694720 | tf_op jit(solution)/shard_map/while/body/eval_jaxpr/jit(_take)/gather | solution.py:85
  613.2 59.6 %gather_fusion.1 = f32[16384,81]{1,0:T(8,128)} fusion(f32[81,2048]{0,1:T(8,128)S(1)} %get-tuple-element.1132, s32[16384]{0:T(1024)} %broadcast_clamp_fusion.2), kind=kCustom, calls=%fused_computation.1.clone.1 | custom fusion | bytes 10682368 | tf_op jit(solution)/shard_map/while/body/eval_jaxpr/jit(_take)/gather | solution.py:84
  672.9 8.2 %copy.91 = f32[16,1024,81]{1,0,2:T(8,128)} copy(f32[16,1024,81]{2,1,0:T(8,128)} %bitcast.287) | data formatting | bytes 10616832 | tf_op jit(solution)/shard_map/while/body/eval_jaxpr/jit(_take)/gather | solution.py:84
  682.0 5.4 multiply_reduce_fusion.55
  708.9 66.9 %gather_fusion = f32[16384,135]{1,0:T(8,128)} fusion(f32[135,2048]{0,1:T(8,128)S(1)} %get-tuple-element.1131, s32[16384]{0:T(1024)} %broadcast_clamp_fusion.2), kind=kCustom, calls=%fused_computation.clone.1 | custom fusion | bytes 17760256 | tf_op jit(solution)/shard_map/while/body/eval_jaxpr/jit(_take)/gather | solution.py:85
  775.8 15.2 %copy.90 = f32[16,1024,135]{1,0,2:T(8,128)} copy(f32[16,1024,135]{2,1,0:T(8,128)} %bitcast.285) | data formatting | bytes 17694720 | tf_op jit(solution)/shard_map/while/body/eval_jaxpr/jit(_take)/gather | solution.py:85
  (274 shorter events, 112.4 us)
Async XLA Ops:
  24.0 22.9 %all-to-all-start.1 = ((s32[64,1,2]{2,1,0:T(1,128)}), s32[64,1,2]{2,1,0:T(1,128)S(1)}, u32[]{:S(2)}, u32[]{:S(2)}) async-start(s32[64,1,2]{2,1,0:T(1,128)} %bitcast.105), calls=%async_computation.1 | async-start | bytes 65536 | tf_op jit(solution)/shard_map/all_to_all | solution.py:120
  59.5 123.8 %all-to-all-start.4 = ((f32[81,64,2,128]{3,2,0,1:T(2,128)}), f32[81,64,2,128]{3,2,0,1:T(2,128)}, u32[]{:S(2)}, u32[]{:S(2)}) async-start(f32[81,64,2,128]{3,2,0,1:T(2,128)} %copy.71), calls=%async_computation.4 | async-start | bytes 10616832 | tf_op jit(solution)/shard_map/all_to_all | solution.py:128
  183.3 200.5 %all-to-all-start.2 = ((f32[135,64,2,128]{3,2,0,1:T(2,128)}), f32[135,64,2,128]{3,2,0,1:T(2,128)}, u32[]{:S(2)}, u32[]{:S(2)}) async-start(f32[135,64,2,128]{3,2,0,1:T(2,128)} %copy.66), calls=%async_computation.2 | async-start | bytes 17694720 | tf_op jit(solution)/shard_map/all_to_all | solution.py:129
  383.9 17.4 %all-to-all-start.5 = ((f32[81,4,4,128]{3,2,0,1:T(4,128)}), f32[81,4,4,128]{3,2,0,1:T(4,128)S(1)}, u32[]{:S(2)}, u32[]{:S(2)}) async-start(f32[81,4,4,128]{3,2,0,1:T(4,128)} %copy.73), calls=%async_computation.5 | async-start | bytes 1327104 | tf_op jit(solution)/shard_map/all_to_all | solution.py:136
  399.9 15.8 %copy-start.4 = (s32[16,2048]{1,0:T(8,128)S(1)}, s32[16,2048]{1,0:T(8,128)}, u32[]{:S(2)}) copy-start(s32[16,2048]{1,0:T(8,128)} %param.12) | copy-start | bytes 393220
  401.2 15.6 %all-to-all-start.3 = ((f32[135,4,4,128]{3,2,0,1:T(4,128)}), f32[135,4,4,128]{3,2,0,1:T(4,128)}, u32[]{:S(2)}, u32[]{:S(2)}) async-start(f32[135,4,4,128]{3,2,0,1:T(4,128)} %copy.68), calls=%async_computation.3 | async-start | bytes 2211840 | tf_op jit(solution)/shard_map/all_to_all | solution.py:137
  416.8 2.5 copy-start
  416.8 2.5 copy-start.1
  493.0 5.4 copy-start.3
  499.0 2.2 slice-start
  499.3 2.3 slice-start.1
  602.1 5.4 copy-start.2
  682.0 5.4 copy-start.3
  687.9 2.2 slice-start
  688.2 2.3 slice-start.1
  791.0 5.4 copy-start.2
where the time goes:
time: 811 us; the launch traced here: 797 us
  local copies, waits for them, and re-layouts  368 us (45%)
  waiting for transfers between devices  286 us (35%)
  other arithmetic  97.8 us (12%)
  starting transfers between devices  35.1 us (4%)
  blocking collectives  8.94 us (1%)
    all_to_all x1, waiting for transfers between devices, local(): lax.all_to_all(flow_rows, 'dom', split_axis=1, concat_axis=1, tiled=True)  183 us
    gather x4, local copies, waits for them, and re-layouts, advance(): values = jnp.take(flows, ids, axis=1)  164 us
    gather x4, local copies, waits for them, and re-layouts, advance(): cells = jnp.take(nodes, ids, axis=1)  136 us
    all_to_all x1, waiting for transfers between devices, local(): lax.all_to_all(node_rows, 'dom', split_axis=1, concat_axis=1, tiled=True)  96.1 us
    reduce_sum x12, other arithmetic, blend_points(): column_z = jnp.sum(geometry * along_z[None], axis=1)  27.9 us
    mul x28, other arithmetic, tensor_basis(): joined = first[:, None, None] * second[None, :, None] * third[None, None, :]  21.1 us
  transfers between devices with their start and end apart: 5, of which 3 were waited for; matrix products, arithmetic and copies ran while one was open for 7% of the time, Pallas kernels for 0%

commit v1 on v0

v1 whole, which is shorter than its diff:
```python
import functools

import jax
import jax.numpy as jnp
import numpy as np
from jax import lax
from jax.experimental import pallas as pl
from jax.experimental.pallas import tpu as pltpu
from jax.sharding import PartitionSpec as P

VARS = 5
LANES = 128
STEPS = 6
CAP_DOM = 2

clamp_edge = 1.25
relax_factor = 0.5
sharpness = 16.0

MESH = pl.DeviceIdType.MESH
F32 = jnp.float32
I32 = jnp.int32


def monomial_map(fields):
    one = np.array([[0.0, 1.0, 0.0], [-0.5, 0.0, 0.5], [0.5, -1.0, 0.5]])
    cell = np.kron(np.kron(one, one), one)
    return np.kron(np.eye(fields), cell).astype(np.float32)


def enter(bins, doms):
    me_dom, me_bin = lax.axis_index("dom"), lax.axis_index("bin")
    barrier = pltpu.get_barrier_semaphore()

    def greet_bin(off, carry):
        other = lax.rem(me_bin + off, bins)
        pl.semaphore_signal(barrier, inc=1, device_id=(me_dom, other), device_id_type=MESH)
        return carry

    def greet_dom(off, carry):
        other = lax.rem(me_dom + off, doms)
        pl.semaphore_signal(barrier, inc=1, device_id=(other, me_bin), device_id_type=MESH)
        return carry

    lax.fori_loop(1, bins, greet_bin, 0)
    lax.fori_loop(1, doms, greet_dom, 0)
    return lambda: pl.semaphore_wait(barrier, bins - 1 + doms - 1)


def exchange(count, copy_to):
    def start(off, carry):
        copy_to(off).start()
        return carry

    def finish(off, carry):
        copy_to(off).wait()
        return carry

    lax.fori_loop(1, count, start, 0)
    return lambda: lax.fori_loop(1, count, finish, 0)


def ranks(labels):
    count = len(labels)
    out = []
    for i in range(count):
        rank = jnp.int32(0)
        for j in range(i):
            rank = rank + (labels[j] == labels[i]).astype(I32)
        out.append(rank)
    return out


def request_kernel(
    bins, doms, blocks,
    bin_ref, dom_ref, slot_ref, pts_ref, cand_ref,
    tiles_ref, meta_ref,
    raw, msg, got, pack, bin_send, bin_recv, dom_send, dom_recv,
):
    me_dom, me_bin = lax.axis_index("dom"), lax.axis_index("bin")
    per = blocks // bins
    entered = enter(bins, doms)
    sub = lax.broadcasted_iota(I32, (8, LANES), 0)
    lane = lax.broadcasted_iota(I32, (8, LANES), 1)

    for b in range(blocks):
        span = pl.ds(b * LANES, LANES)
        corner = jnp.min(cand_ref[:, span], axis=0, keepdims=True)
        raw[b, 0:3, :] = pts_ref[:, span]
        raw[b, 3:4, :] = (corner + slot_ref[b] * LANES).astype(F32)
        raw[b, 4:5, :] = jnp.full((1, LANES), dom_ref[b], I32).astype(F32)
        raw[b, 5:8, :] = jnp.zeros((3, LANES), F32)
    bin_of = [bin_ref[b] for b in range(blocks)]
    place = [x * per + r for x, r in zip(bin_of, ranks(bin_of))]
    for p in range(blocks):
        source = jnp.int32(0)
        for b in range(blocks):
            source = source + jnp.where(place[b] == p, b, 0)
        msg[p] = raw[source]
    entered()

    def to_bin(off):
        other = lax.rem(me_bin + off, bins)
        return pltpu.make_async_remote_copy(
            src_ref=msg.at[pl.ds(other * per, per)],
            dst_ref=got.at[pl.ds(me_bin * per, per)],
            send_sem=bin_send.at[off],
            recv_sem=bin_recv.at[off],
            device_id=(me_dom, other),
            device_id_type=MESH,
        )

    finish = exchange(bins, to_bin)
    for i in range(per):
        got[me_bin * per + i] = msg[me_bin * per + i]
    finish()

    named, tiles, number = [], [], []
    for b in range(blocks):
        tile = got[b]
        name = jnp.broadcast_to(got[b, 4:5, :], (8, LANES))
        rank = jnp.zeros((8, LANES), F32)
        for j in range(b):
            rank = rank + jnp.where(number[j] == name, 1.0, 0.0)
        number.append(name)
        named.append(jnp.where(jnp.where(sub < 4, 0.0, 1.0) == rank, name, -1.0))
        tiles.append(jnp.where(sub < 4, tile, pltpu.roll(tile, 4, 0)))
        number_rank = (name * CAP_DOM + rank).astype(I32)
        if b == 0:
            where_row = jnp.where(lane == 0, number_rank, 0)
        else:
            where_row = jnp.where(lane == b, number_rank, where_row)
    empty = jnp.where(sub % 4 == 3, -1.0, 0.0)

    def fill(a, carry):
        target = a.astype(F32)
        acc = empty
        for b in range(blocks):
            acc = jnp.where(named[b] == target, tiles[b], acc)
        pack[a] = acc
        return carry

    lax.fori_loop(0, doms, fill, 0)

    def to_dom(off):
        other = lax.rem(me_dom + off, doms)
        return pltpu.make_async_remote_copy(
            src_ref=pack.at[other],
            dst_ref=tiles_ref.at[me_dom],
            send_sem=dom_send.at[off],
            recv_sem=dom_recv.at[off],
            device_id=(other, me_bin),
            device_id_type=MESH,
        )

    finish = exchange(doms, to_dom)
    tiles_ref[me_dom] = pack[me_dom]
    finish()

    def table(a, acc):
        tile = tiles_ref[a]
        for k in range(CAP_DOM):
            cell = jnp.broadcast_to(tile[4 * k + 3 : 4 * k + 4, :], (8, LANES))
            slot = jnp.floor(cell * (1.0 / LANES)).astype(I32)
            acc = jnp.where(lane == CAP_DOM * a + k, slot, acc)
        return acc

    slots = lax.fori_loop(0, doms, table, jnp.full((8, LANES), -1, I32))
    meta_ref[...] = jnp.where(sub == 0, slots, jnp.where(sub == 1, where_row, 0))


def horner(t, c0, c1, c2):
    return (c2 * t + c1) * t + c0


def horner_slope(t, c0, c1, c2):
    top = c2 * t
    mid = top + c1
    return mid * t + c0, mid + top


def cross(a, b):
    return (
        a[1] * b[2] - a[2] * b[1],
        a[2] * b[0] - a[0] * b[2],
        a[0] * b[1] - a[1] * b[0],
    )


def dot3(a, b):
    return a[0] * b[0] + a[1] * b[1] + a[2] * b[2]


def blend_kernel(
    requests, cells,
    meta_ref, tiles_ref, node_map_ref, flow_map_ref, nodes_ref, flow_ref,
    out_ref,
    node_c, flow_c, held,
):
    width = 256

    def convert(i, carry):
        span = pl.ds(pl.multiple_of(i * width, width), width)
        node_c[:, span] = jnp.dot(
            node_map_ref[...], nodes_ref[:, span],
            precision=lax.Precision.HIGHEST, preferred_element_type=F32,
        )
        flow_c[:, span] = jnp.dot(
            flow_map_ref[...], flow_ref[:, span],
            precision=lax.Precision.HIGHEST, preferred_element_type=F32,
        )
        return carry

    lax.fori_loop(0, cells // width, convert, 0)

    row = lax.broadcasted_iota(I32, (8, LANES), 0)
    box = 8 * (row // 4) + row % 4

    def one(number, slot):
        base = lax.rem(number, CAP_DOM) * 4
        tile = number // CAP_DOM
        points = [
            jnp.broadcast_to(tiles_ref[tile, pl.ds(base + c, 1), :], (16, LANES)) for c in range(3)
        ]
        cell = tiles_ref[tile, pl.ds(base + 3, 1), :]
        corner = jnp.broadcast_to(cell.astype(I32) - slot * LANES, (8, LANES)) + box
        halves = (corner, corner + 32)
        span = pl.ds(pl.multiple_of(slot * LANES, LANES), LANES)

        def pick(table, r):
            line = jnp.broadcast_to(table[r : r + 1, span], (8, LANES))
            return jnp.concatenate(
                [jnp.take_along_axis(line, h, axis=1, mode="promise_in_bounds") for h in halves],
                axis=0,
            )

        for r in range(81):
            held[r] = pick(node_c, r)

        def coeff(c, i, j, k):
            return held[27 * c + 9 * i + 3 * j + k]

        r = None
        for step in range(STEPS):
            value, d1, d2, d3 = [], [], [], []
            for c in range(3):
                if r is None:
                    value.append(coeff(c, 0, 0, 0))
                    d1.append(coeff(c, 1, 0, 0))
                    d2.append(coeff(c, 0, 1, 0))
                    d3.append(coeff(c, 0, 0, 1))
                    continue
                x0, x2, x3 = [], [], []
                for i in range(3):
                    y0, y3 = [], []
                    for j in range(3):
                        v, d = horner_slope(r[2], *[coeff(c, i, j, k) for k in range(3)])
                        y0.append(v)
                        y3.append(d)
                    v, d = horner_slope(r[1], *y0)
                    x0.append(v)
                    x2.append(d)
                    x3.append(horner(r[1], *y3))
                v, d = horner_slope(r[0], *x0)
                value.append(v)
                d1.append(d)
                d2.append(horner(r[0], *x2))
                d3.append(horner(r[0], *x3))
            misfit = [value[c] - points[c] for c in range(3)]
            normal = cross(d2, d3)
            side = cross(d1, misfit)
            scale = relax_factor / dot3(d1, normal)
            change = (dot3(misfit, normal), dot3(d3, side), -dot3(d2, side))
            r = [
                jnp.clip((0.0 if r is None else r[c]) - scale * change[c], -clamp_edge, clamp_edge)
                for c in range(3)
            ]
        excess = [jnp.maximum(jnp.abs(x) - 1.0, 0.0) for x in r]
        trust = 1.0 / (1.0 + sharpness * dot3(excess, excess))
        total = 1.0 / jnp.sum(trust, axis=0, keepdims=True)
        for v in range(VARS):
            x0 = []
            for i in range(3):
                y0 = []
                for j in range(3):
                    y0.append(
                        horner(r[2], *[pick(flow_c, 27 * v + 9 * i + 3 * j + k) for k in range(3)])
                    )
                x0.append(horner(r[1], *y0))
            field = horner(r[0], *x0)
            out_ref[number, v : v + 1, :] = jnp.sum(field * trust, axis=0, keepdims=True) * total

    def each(i, carry):
        slot = meta_ref[0, i]

        @pl.when(slot >= 0)
        def _():
            one(i, slot)

        return carry

    lax.fori_loop(0, requests, each, 0)


def reply_kernel(
    bins, doms, blocks,
    bin_ref, meta_ref, res_ref,
    out_ref,
    back, picked, final, bin_send, bin_recv, dom_send, dom_recv,
):
    me_dom, me_bin = lax.axis_index("dom"), lax.axis_index("bin")
    per = blocks // bins
    entered = enter(bins, doms)
    entered()

    def to_dom(off):
        other = lax.rem(me_dom + off, doms)
        return pltpu.make_async_remote_copy(
            src_ref=res_ref.at[pl.ds(CAP_DOM * other, CAP_DOM)],
            dst_ref=back.at[pl.ds(CAP_DOM * me_dom, CAP_DOM)],
            send_sem=dom_send.at[off],
            recv_sem=dom_recv.at[off],
            device_id=(other, me_bin),
            device_id_type=MESH,
        )

    finish = exchange(doms, to_dom)
    for k in range(CAP_DOM):
        back[CAP_DOM * me_dom + k] = res_ref[CAP_DOM * me_dom + k]
    finish()
    for b in range(blocks):
        picked[b] = back[meta_ref[1, b]]

    def to_bin(off):
        other = lax.rem(me_bin + off, bins)
        return pltpu.make_async_remote_copy(
            src_ref=picked.at[pl.ds(other * per, per)],
            dst_ref=final.at[pl.ds(me_bin * per, per)],
            send_sem=bin_send.at[off],
            recv_sem=bin_recv.at[off],
            device_id=(me_dom, other),
            device_id_type=MESH,
        )

    finish = exchange(bins, to_bin)
    for i in range(per):
        final[me_bin * per + i] = picked[me_bin * per + i]
    finish()
    bin_of = [bin_ref[b] for b in range(blocks)]
    place = [x * per + r for x, r in zip(bin_of, ranks(bin_of))]
    for b in range(blocks):
        out_ref[:, pl.ds(b * LANES, LANES)] = final[place[b]][0:VARS, :]


def local(points, candidates, block_dom, block_bin, block_slot, donor_nodes, donor_flow):
    bins, doms = lax.axis_size("bin"), lax.axis_size("dom")
    blocks = block_dom.shape[0]
    requests = doms * CAP_DOM
    cells = donor_nodes.shape[1]
    vmem = pl.BlockSpec(memory_space=pltpu.VMEM)
    smem = pl.BlockSpec(memory_space=pltpu.SMEM)
    sems = [
        pltpu.SemaphoreType.DMA((bins,)),
        pltpu.SemaphoreType.DMA((bins,)),
        pltpu.SemaphoreType.DMA((doms,)),
        pltpu.SemaphoreType.DMA((doms,)),
    ]

    tiles, meta = pl.pallas_call(
        functools.partial(request_kernel, bins, doms, blocks),
        out_shape=(
            jax.ShapeDtypeStruct((doms, 8, LANES), F32),
            jax.ShapeDtypeStruct((8, LANES), I32),
        ),
        in_specs=[smem, smem, smem, vmem, vmem],
        out_specs=(vmem, vmem),
        scratch_shapes=[
            pltpu.VMEM((blocks, 8, LANES), F32),
            pltpu.VMEM((blocks, 8, LANES), F32),
            pltpu.VMEM((blocks, 8, LANES), F32),
            pltpu.VMEM((doms, 8, LANES), F32),
            *sems,
        ],
        compiler_params=pltpu.CompilerParams(collective_id=0, has_side_effects=True),
        name="request",
    )(block_bin, block_dom, block_slot, points, candidates)

    result = pl.pallas_call(
        functools.partial(blend_kernel, requests, cells),
        out_shape=jax.ShapeDtypeStruct((requests, 8, LANES), F32),
        in_specs=[smem, vmem, vmem, vmem, vmem, vmem],
        out_specs=vmem,
        scratch_shapes=[
            pltpu.VMEM((81, cells), F32),
            pltpu.VMEM((135, cells), F32),
            pltpu.VMEM((81, 16, LANES), F32),
        ],
        name="blend",
    )(
        meta, tiles, jnp.asarray(monomial_map(3)), jnp.asarray(monomial_map(VARS)),
        donor_nodes, donor_flow,
    )

    return pl.pallas_call(
        functools.partial(reply_kernel, bins, doms, blocks),
        out_shape=jax.ShapeDtypeStruct((VARS, points.shape[1]), F32),
        in_specs=[smem, smem, vmem],
        out_specs=vmem,
        scratch_shapes=[
            pltpu.VMEM((requests, 8, LANES), F32),
            pltpu.VMEM((blocks, 8, LANES), F32),
            pltpu.VMEM((blocks, 8, LANES), F32),
            *sems,
        ],
        compiler_params=pltpu.CompilerParams(collective_id=1, has_side_effects=True),
        name="reply",
    )(block_bin, meta, result)


def solution(mesh):
    split = P(None, ("dom", "bin"))
    table = P(("dom", "bin"))
    return jax.shard_map(
        local,
        mesh=mesh,
        in_specs=(split, split, table, table, table, split, split),
        out_specs=split,
        check_vma=False,
    )
```

time: 811 us -> 167 us (0.21); the launches traced: 797 us -> 167 us
  local copies, waits for them, and re-layouts: 368 us -> 1.47 us
  waiting for transfers between devices: 286 us -> 0 us
  Pallas kernels: 0 us -> 166 us
  other arithmetic: 97.8 us -> 0 us
  starting transfers between devices: 35.1 us -> 0 us
  blocking collectives: 8.94 us -> 0 us
    gather x15 -> x0, local copies, waits for them, and re-layouts: 317 us -> none  [the longest x4 164 us: advance(): values = jnp.take(flows, ids, axis=1)]
    all_to_all x5 -> x0, waiting for transfers between devices: 286 us -> none  [the longest x1 183 us: local(): lax.all_to_all(flow_rows, 'dom', split_axis=1, concat_axis=1, tiled=True)]
    pallas_call x0 -> x3, Pallas kernels: none -> 166 us  [the longest x1 120 us: local(): pl.pallas_call(functools.partial(reply_kernel, bins, doms, blocks), out_s...]
    reduce_sum x36 -> x0, other arithmetic: 43.1 us -> none  [the longest x12 27.9 us: blend_points(): column_z = jnp.sum(geometry * along_z[None], axis=1)]
    all_to_all x5 -> x0, starting transfers between devices: 35.1 us -> none  [the longest x1 13.6 us: local(): lax.all_to_all(wanted, 'dom', split_axis=0, concat_axis=0, tiled=True)]
    reshape x10 -> x0, local copies, waits for them, and re-layouts: 26.5 us -> none  [the longest x1 13.9 us: local(): flow_rows = flow_rows.reshape(-1, dom_count, per_dom, CELLS_BLK)]
    mul x32 -> x0, other arithmetic: 21.9 us -> none  [the longest x28 21.1 us: tensor_basis(): joined = first[:, None, None] * second[None, :, None] * third[None, None, :]]
    gather x8 -> x0, other arithmetic: 15.8 us -> none  [the longest x1 9.95 us: local(): wanted = route[1][middle_src].reshape(dom_count, per_dom)]
  transfers between devices with their start and end apart: 5 -> 0, of which waited for: 3 -> 0; matrix products, arithmetic and copies ran while one was open for 7% -> 0% of each run, Pallas kernels for 0% -> 0%
where the time goes in v1:
time: 167 us
  Pallas kernels  166 us (99%)
    pallas_call x1, Pallas kernels, local(): pl.pallas_call(functools.partial(reply_kernel, bins, doms, blocks), out_s...  120 us
    pallas_call x1, Pallas kernels, local(): pl.pallas_call(functools.partial(request_kernel, bins, doms, blocks), out...  27.7 us
    pallas_call x1, Pallas kernels, local(): pl.pallas_call(functools.partial(blend_kernel, requests, cells), out_shap...  18.3 us

profile of v1, /device:TPU:1, one launch (start us, length us, event | category | flops | bytes accessed | tf_op | source)
XLA Modules:
  0.0 167.3 jit_solution(8973239468531907859)
XLA Ops:
  0.0 27.7 %request.1 = (f32[64,8,128]{2,1,0:T(8,128)}, s32[8,128]{1,0:T(8,128)}) custom-call(s32[16]{0:T(128)} %bin_ref.3, s32[16]{0:T(128)} %dom_ref.1, s32[16]{0:T(128)} %slot_ref.1, f32[3,2048]{1,0:T(4,128)} %pts_ref.1, s32[16,2048]{1,0:T(8,128)} %cand_ref.1), custom_call_target="tpu_custom_call" | custom-call | tf_op jit(solution)/shard_map/request/pallas_call | solution.py:369
  27.8 18.3 %blend.1.res_ref = f32[128,8,128]{2,1,0:T(8,128)} custom-call(s32[8,128]{1,0:T(8,128)} %get-tuple-element.7.meta_ref, f32[64,8,128]{2,1,0:T(8,128)} %get-tuple-element.8.tiles_ref, f32[81,81]{1,0:T(8,128)} %constant.4.clone.node_map_ref, f32[135,135]{1,0:T(8,128)} %constant.5.clone.flow_map_ref, f32[81,4096]{1,0:T(8,128)} %nodes_ref.1, f32[135,4096]{1,0:T(8,128)} %flow_ref.1), custom_call_target="tpu_custom_call" | custom-call | tf_op jit(solution)/shard_map/blend/pallas_call | solution.py:388
  46.0 119.8 %reply.1 = f32[5,2048]{1,0:T(8,128)} custom-call(s32[16]{0:T(128)} %bin_ref.3, s32[8,128]{1,0:T(8,128)} %get-tuple-element.7.meta_ref, f32[128,8,128]{2,1,0:T(8,128)} %blend.1.res_ref), custom_call_target="tpu_custom_call" | custom-call | tf_op jit(solution)/shard_map/reply/pallas_call | solution.py:404
  165.8 1.5 copy.11

commit v2 on v1

v2 whole, which is shorter than its diff:
```python
import functools

import jax
import jax.numpy as jnp
import numpy as np
from jax import lax
from jax.experimental import pallas as pl
from jax.experimental.pallas import tpu as pltpu
from jax.sharding import PartitionSpec as P

VARS = 5
LANES = 128
STEPS = 6
CAP_DOM = 2
X_CHIPS, CORES = 4, 2

UNIT = 16
NEAR = 6
SPREAD = NEAR * CORES
GUEST = SPREAD + 2
NODE_ROWS, FLOW_ROWS = 88, 136
ROWS = NODE_ROWS + FLOW_ROWS

clamp_edge = 1.25
relax_factor = 0.5
sharpness = 16.0

MESH = pl.DeviceIdType.MESH
F32 = jnp.float32
I32 = jnp.int32


def monomial_map(fields, rows):
    one = np.array([[0.0, 1.0, 0.0], [-0.5, 0.0, 0.5], [0.5, -1.0, 0.5]])
    cell = np.kron(np.kron(one, one), one)
    full = np.kron(np.eye(fields), cell)
    return np.pad(full, ((0, rows - full.shape[0]), (0, 0)))


def exact_dot(left, right):
    high = right.astype(jnp.bfloat16)
    rest = right - high.astype(F32)
    mid = rest.astype(jnp.bfloat16)
    low = (rest - mid.astype(F32)).astype(jnp.bfloat16)
    out = jnp.dot(left, low, preferred_element_type=F32)
    out = out + jnp.dot(left, mid, preferred_element_type=F32)
    return out + jnp.dot(left, high, preferred_element_type=F32)


class Place:
    def __init__(self, bins, doms):
        self.bins, self.doms = bins, doms
        self.dom, self.bin = lax.axis_index("dom"), lax.axis_index("bin")
        self.core = lax.rem(self.dom, CORES)
        self.x = lax.rem(self.dom // CORES, X_CHIPS)
        self.z = self.dom // (CORES * X_CHIPS)

    def chip(self, near, core, sign=1):
        step = sign if near % 2 == 0 else -sign
        layers = self.doms // (CORES * X_CHIPS)
        z, x, y = self.z, self.x, self.bin
        if near // 2 == 0:
            z = lax.rem(z + step + layers, layers)
        elif near // 2 == 1:
            x = lax.rem(x + step + X_CHIPS, X_CHIPS)
        else:
            y = lax.rem(y + step + self.bins, self.bins)
        return ((z * X_CHIPS + x) * CORES + core, y)

    def sibling(self):
        return (self.dom + 1 - 2 * self.core, self.bin)

    def enter(self):
        barrier = pltpu.get_barrier_semaphore()

        def greet(device):
            pl.semaphore_signal(barrier, inc=1, device_id=device, device_id_type=MESH)

        def greet_bin(off, carry):
            greet((self.dom, lax.rem(self.bin + off, self.bins)))
            return carry

        def greet_dom(off, carry):
            greet((lax.rem(self.dom + off, self.doms), self.bin))
            return carry

        lax.fori_loop(1, self.bins, greet_bin, 0)
        lax.fori_loop(1, self.doms, greet_dom, 0)
        for near in (4, 5):
            greet(self.chip(near, 1 - self.core))
        return lambda: pl.semaphore_wait(barrier, self.bins - 1 + self.doms - 1 + 2)


def exchange(count, copy_to):
    def start(off, carry):
        copy_to(off).start()
        return carry

    def finish(off, carry):
        copy_to(off).wait()
        return carry

    lax.fori_loop(1, count, start, 0)
    return lambda: lax.fori_loop(1, count, finish, 0)


def ranks(labels):
    count = len(labels)
    out = []
    for i in range(count):
        rank = jnp.int32(0)
        for j in range(i):
            rank = rank + (labels[j] == labels[i]).astype(I32)
        out.append(rank)
    return out


def request_kernel(
    bins, doms, blocks, cells,
    bin_ref, dom_ref, slot_ref, pts_ref, cand_ref, node_map_ref, flow_map_ref, nodes_ref, flow_ref,
    work_ref, meta_ref, ext_ref, own_ref,
    raw, msg, got, pack, tiles, ship, node_raw, flow_raw, coef,
    load_sem, keep_sem, bin_send, bin_recv, dom_send, dom_recv, ship_send, ship_recv,
    cell_send, cell_recv,
):
    me = Place(bins, doms)
    per = blocks // bins
    parts = load_sem.shape[1]
    width = cells // parts
    step = 256

    def load(i):
        span = pl.ds(i * width, width)
        return (
            pltpu.make_async_copy(nodes_ref.at[:, span], node_raw.at[:, span], load_sem.at[0, i]),
            pltpu.make_async_copy(flow_ref.at[:, span], flow_raw.at[:, span], load_sem.at[1, i]),
        )

    for i in range(parts):
        for copy in load(i):
            copy.start()
    entered = me.enter()
    sub = lax.broadcasted_iota(I32, (8, LANES), 0)
    lane = lax.broadcasted_iota(I32, (8, LANES), 1)

    for b in range(blocks):
        span = pl.ds(b * LANES, LANES)
        corner = jnp.min(cand_ref[:, span], axis=0, keepdims=True)
        raw[b, 0:3, :] = pts_ref[:, span]
        raw[b, 3:4, :] = (corner + slot_ref[b] * LANES).astype(F32)
        raw[b, 4:5, :] = jnp.full((1, LANES), dom_ref[b], I32).astype(F32)
        raw[b, 5:8, :] = jnp.zeros((3, LANES), F32)
    bin_of = [bin_ref[b] for b in range(blocks)]
    place = [x * per + r for x, r in zip(bin_of, ranks(bin_of))]
    for p in range(blocks):
        source = jnp.int32(0)
        for b in range(blocks):
            source = source + jnp.where(place[b] == p, b, 0)
        msg[p] = raw[source]

    def convert(i, carry):
        span = pl.ds(pl.multiple_of(i * step, step), step)
        node = exact_dot(node_map_ref[...], node_raw[:, span])
        flow = exact_dot(flow_map_ref[...], flow_raw[:, span])
        for k in range(step // LANES):
            part = slice(k * LANES, (k + 1) * LANES)
            coef[i * (step // LANES) + k, 0:NODE_ROWS, :] = node[:, part]
            coef[i * (step // LANES) + k, NODE_ROWS:ROWS, :] = flow[:, part]
        return carry

    for i in range(parts):
        for copy in load(i):
            copy.wait()
        lax.fori_loop(i * width // step, (i + 1) * width // step, convert, 0)
    keep = [
        pltpu.make_async_copy(coef, own_ref, keep_sem.at[0]),
        pltpu.make_async_copy(coef.at[0:4], ext_ref.at[0:4], keep_sem.at[1]),
    ]
    entered()

    def to_bin(off):
        other = lax.rem(me.bin + off, bins)
        return pltpu.make_async_remote_copy(
            src_ref=msg.at[pl.ds(other * per, per)],
            dst_ref=got.at[pl.ds(me.bin * per, per)],
            send_sem=bin_send.at[off],
            recv_sem=bin_recv.at[off],
            device_id=(me.dom, other),
            device_id_type=MESH,
        )

    finish_bin = exchange(bins, to_bin)

    spread = []
    for unit in range(SPREAD):
        near, core = unit // CORES, unit % CORES
        spread.append(
            pltpu.make_async_remote_copy(
                src_ref=coef.at[pl.ds(8 + 2 * unit, 2)],
                dst_ref=ext_ref.at[pl.ds(8 + 2 * (near * CORES + me.core), 2)],
                send_sem=cell_send.at[unit],
                recv_sem=cell_recv.at[near * CORES + me.core],
                device_id=me.chip(near, core),
                device_id_type=MESH,
            )
        )
    spread.append(
        pltpu.make_async_remote_copy(
            src_ref=coef.at[4:8],
            dst_ref=ext_ref.at[4:8],
            send_sem=cell_send.at[SPREAD],
            recv_sem=cell_recv.at[SPREAD],
            device_id=me.sibling(),
            device_id_type=MESH,
        )
    )
    for copy in spread:
        copy.start()
    for copy in keep:
        copy.start()

    for i in range(per):
        got[me.bin * per + i] = msg[me.bin * per + i]
    finish_bin()

    named, tile_of, number = [], [], []
    where_row = jnp.zeros((8, LANES), I32)
    for b in range(blocks):
        tile = got[b]
        name = jnp.broadcast_to(got[b, 4:5, :], (8, LANES))
        rank = jnp.zeros((8, LANES), F32)
        for j in range(b):
            rank = rank + jnp.where(number[j] == name, 1.0, 0.0)
        number.append(name)
        named.append(jnp.where(jnp.where(sub < 4, 0.0, 1.0) == rank, name, -1.0))
        tile_of.append(jnp.where(sub < 4, tile, pltpu.roll(tile, 4, 0)))
        where_row = jnp.where(lane == b, (name * CAP_DOM + rank).astype(I32), where_row)
    empty = jnp.where(sub % 4 == 3, -1.0, 0.0)

    def fill(a, carry):
        target = a.astype(F32)
        acc = empty
        for b in range(blocks):
            acc = jnp.where(named[b] == target, tile_of[b], acc)
        pack[a] = acc
        return carry

    lax.fori_loop(0, doms, fill, 0)

    def to_dom(off):
        other = lax.rem(me.dom + off, doms)
        return pltpu.make_async_remote_copy(
            src_ref=pack.at[other],
            dst_ref=tiles.at[pl.ds(pl.multiple_of(8 * me.dom, 8), 8)],
            send_sem=dom_send.at[off],
            recv_sem=dom_recv.at[off],
            device_id=(other, me.bin),
            device_id_type=MESH,
        )

    finish_dom = exchange(doms, to_dom)
    tiles[pl.ds(pl.multiple_of(8 * me.dom, 8), 8), :] = pack[me.dom]
    finish_dom()

    count = doms * CAP_DOM
    square = (count, LANES)
    row = [tiles[pl.ds(c, count, stride=4), :] for c in range(4)]
    first = lax.broadcasted_iota(I32, square, 0)
    second = lax.broadcasted_iota(I32, square, 1)
    before = first < second
    slot = jnp.floor(row[3] * (1.0 / LANES)).astype(I32)
    base = jnp.where(slot < 4, GUEST, jnp.where(slot < 8, SPREAD, (slot - 8) // 2))
    base = jnp.where(slot < 0, -1, base).astype(F32)
    base_row = base.T
    rank = jnp.sum(jnp.where((base == base_row) & before, 1.0, 0.0), axis=0, keepdims=True)
    base_row = base_row[0:1, :]
    cap = jnp.where(base_row == SPREAD, 2.0 * UNIT, 1.0 * UNIT)
    stay = (base_row == GUEST) | ((base_row >= 0.0) & (rank >= cap))
    stay_row = jnp.where(stay, 1.0, 0.0)
    stay_col = jnp.broadcast_to(stay_row, square).T
    stay_rank = jnp.sum(jnp.where(before, stay_col, 0.0), axis=0, keepdims=True)
    target = jnp.where(stay, GUEST * UNIT + stay_rank, base_row * UNIT + rank)
    target = jnp.where(base_row < 0.0, -1.0, target).astype(I32)
    places = GUEST * UNIT + count
    units = places // UNIT
    hot = jnp.where(
        lax.broadcasted_iota(I32, (places, LANES), 0) == jnp.broadcast_to(target, (places, LANES)),
        1.0, 0.0,
    ).astype(jnp.bfloat16)
    for c in range(4):
        moved = exact_dot(hot, row[c] + 1.0 if c == 3 else row[c])
        if c == 3:
            moved = moved - 1.0
        for u in range(GUEST):
            ship[u, c] = moved[u * UNIT : (u + 1) * UNIT, :]
        for u in range(GUEST, units):
            work_ref[u, c] = moved[u * UNIT : (u + 1) * UNIT, :]

    shipped = []
    for unit in range(SPREAD):
        near, core = unit // CORES, unit % CORES
        shipped.append(
            pltpu.make_async_remote_copy(
                src_ref=ship.at[unit],
                dst_ref=work_ref.at[near * CORES + me.core],
                send_sem=ship_send.at[unit],
                recv_sem=ship_recv.at[near * CORES + me.core],
                device_id=me.chip(near, core),
                device_id_type=MESH,
            )
        )
    shipped.append(
        pltpu.make_async_remote_copy(
            src_ref=ship.at[pl.ds(SPREAD, 2)],
            dst_ref=work_ref.at[pl.ds(SPREAD, 2)],
            send_sem=ship_send.at[SPREAD],
            recv_sem=ship_recv.at[SPREAD],
            device_id=me.sibling(),
            device_id_type=MESH,
        )
    )
    for copy in shipped:
        copy.start()

    def arrived(unit, sem, ref):
        return pltpu.make_async_remote_copy(
            src_ref=ref, dst_ref=ref, send_sem=sem.at[unit], recv_sem=sem.at[unit],
            device_id=me.sibling(), device_id_type=MESH,
        ).wait_recv()

    for unit in range(SPREAD):
        arrived(unit, ship_recv, work_ref.at[unit])
    arrived(SPREAD, ship_recv, work_ref.at[pl.ds(SPREAD, 2)])

    tall = (UNIT, LANES)
    down, across = lax.broadcasted_iota(I32, tall, 0), lax.broadcasted_iota(I32, tall, 1)
    lines = [jnp.zeros(tall, I32) for _ in range(3)]
    for u in range(units):
        slot = jnp.floor(work_ref[u, 3] * (1.0 / LANES)).astype(I32)
        if u < SPREAD:
            block = slot + 2 * (u % CORES - me.core)
        elif u < GUEST:
            block = slot
        else:
            block = jnp.where(slot < 4, slot, slot + 32)
        block = jnp.where(slot < 0, 0, block + 1)
        line = u * UNIT // LANES
        lines[line] = lines[line] + jnp.where(across == (u * UNIT) % LANES + down, block, 0)
    table = jnp.where(sub == 3, jnp.broadcast_to(target, sub.shape), where_row)
    for i in range(3):
        total = jnp.sum(lines[i].astype(F32), axis=0, keepdims=True).astype(I32) - 1
        table = jnp.where(sub == i, jnp.broadcast_to(total, sub.shape), table)
    meta_ref[...] = table

    for copy in shipped + spread:
        copy.wait_send()
    for unit in range(SPREAD):
        arrived(unit, cell_recv, ext_ref.at[pl.ds(8 + 2 * unit, 2)])
    arrived(SPREAD, cell_recv, ext_ref.at[4:8])
    for copy in keep:
        copy.wait()


def horner(t, c0, c1, c2):
    return (c2 * t + c1) * t + c0


def horner_slope(t, c0, c1, c2):
    top = c2 * t
    mid = top + c1
    return mid * t + c0, mid + top


def cross(a, b):
    return (
        a[1] * b[2] - a[2] * b[1],
        a[2] * b[0] - a[0] * b[2],
        a[0] * b[1] - a[1] * b[0],
    )


def dot3(a, b):
    return a[0] * b[0] + a[1] * b[1] + a[2] * b[2]


def blend_kernel(
    places, total_places,
    meta_ref, work_ref, ext_ref, own_ref,
    out_ref,
    held, buf, order, sem,
):
    def collect(first, last, found):
        def more(state):
            i, n = state
            at = jnp.minimum(i, total_places - 1)
            return (i < last) & (meta_ref[at // LANES, lax.rem(at, LANES)] >= 0)

        def note(state):
            i, n = state
            order[n] = i
            return i + 1, n + 1

        return lax.while_loop(more, note, (jnp.int32(first), found))[1]

    found = jnp.int32(0)
    for u in range(SPREAD):
        found = collect(u * UNIT, (u + 1) * UNIT, found)
    found = collect(SPREAD * UNIT, GUEST * UNIT, found)
    found = collect(GUEST * UNIT, total_places, found)

    def fetch(n, act):
        at = order[n]
        block = meta_ref[at // LANES, lax.rem(at, LANES)]
        side = lax.rem(n, 2)

        @pl.when(block < 32)
        def _():
            act(pltpu.make_async_copy(ext_ref.at[block], buf.at[side], sem.at[side]))

        @pl.when(block >= 32)
        def _():
            act(pltpu.make_async_copy(own_ref.at[block - 32], buf.at[side], sem.at[side]))

    @pl.when(found > 0)
    def _():
        fetch(0, lambda copy: copy.start())

    row = lax.broadcasted_iota(I32, (8, LANES), 0)
    box = 8 * (row // 4) + row % 4

    def one(n, carry):
        @pl.when(n + 1 < found)
        def _():
            fetch(n + 1, lambda copy: copy.start())

        fetch(n, lambda copy: copy.wait())
        place = order[n]
        half = lax.rem(n, 2)
        unit, at = place // UNIT, lax.rem(place, UNIT)
        points = [
            jnp.broadcast_to(work_ref[unit, c, pl.ds(at, 1), :], (16, LANES)) for c in range(3)
        ]
        cell = work_ref[unit, 3, pl.ds(at, 1), :].astype(I32) & (LANES - 1)
        corner = jnp.broadcast_to(cell, (8, LANES)) + box
        halves = (corner, corner + 32)

        def pick(r):
            line = jnp.broadcast_to(buf[half, r : r + 1, :], (8, LANES))
            return jnp.concatenate(
                [jnp.take_along_axis(line, h, axis=1, mode="promise_in_bounds") for h in halves],
                axis=0,
            )

        for r in range(81):
            held[r] = pick(r)

        def coeff(c, i, j, k):
            return held[27 * c + 9 * i + 3 * j + k]

        r = None
        for step in range(STEPS):
            value, d1, d2, d3 = [], [], [], []
            for c in range(3):
                if r is None:
                    value.append(coeff(c, 0, 0, 0))
                    d1.append(coeff(c, 1, 0, 0))
                    d2.append(coeff(c, 0, 1, 0))
                    d3.append(coeff(c, 0, 0, 1))
                    continue
                x0, x2, x3 = [], [], []
                for i in range(3):
                    y0, y3 = [], []
                    for j in range(3):
                        v, d = horner_slope(r[2], *[coeff(c, i, j, k) for k in range(3)])
                        y0.append(v)
                        y3.append(d)
                    v, d = horner_slope(r[1], *y0)
                    x0.append(v)
                    x2.append(d)
                    x3.append(horner(r[1], *y3))
                v, d = horner_slope(r[0], *x0)
                value.append(v)
                d1.append(d)
                d2.append(horner(r[0], *x2))
                d3.append(horner(r[0], *x3))
            misfit = [value[c] - points[c] for c in range(3)]
            normal = cross(d2, d3)
            side = cross(d1, misfit)
            scale = relax_factor / dot3(d1, normal)
            change = (dot3(misfit, normal), dot3(d3, side), -dot3(d2, side))
            r = [
                jnp.clip((0.0 if r is None else r[c]) - scale * change[c], -clamp_edge, clamp_edge)
                for c in range(3)
            ]
        excess = [jnp.maximum(jnp.abs(x) - 1.0, 0.0) for x in r]
        trust = 1.0 / (1.0 + sharpness * dot3(excess, excess))
        total = 1.0 / jnp.sum(trust, axis=0, keepdims=True)
        for v in range(VARS):
            x0 = []
            for i in range(3):
                y0 = []
                for j in range(3):
                    y0.append(
                        horner(r[2], *[pick(NODE_ROWS + 27 * v + 9 * i + 3 * j + k) for k in range(3)])
                    )
                x0.append(horner(r[1], *y0))
            field = horner(r[0], *x0)
            out_ref[place, v] = jnp.sum(field * trust, axis=0, keepdims=True) * total
        return carry

    lax.fori_loop(0, found, one, 0)


def reply_kernel(
    bins, doms, blocks,
    bin_ref, meta_ref, res_ref,
    out_ref,
    ret, send, back, picked, final,
    keep_sem, bin_send, bin_recv, dom_send, dom_recv, ship_send, ship_recv,
):
    me = Place(bins, doms)
    per = blocks // bins
    count = doms * CAP_DOM
    entered = me.enter()
    keep = pltpu.make_async_copy(
        res_ref.at[pl.ds(GUEST * UNIT, count)], ret.at[pl.ds(GUEST * UNIT, count)], keep_sem
    )
    keep.start()
    entered()

    shipped = []
    for unit in range(SPREAD):
        near, core = unit // CORES, unit % CORES
        shipped.append(
            pltpu.make_async_remote_copy(
                src_ref=res_ref.at[pl.ds(unit * UNIT, UNIT)],
                dst_ref=ret.at[pl.ds((near * CORES + me.core) * UNIT, UNIT)],
                send_sem=ship_send.at[unit],
                recv_sem=ship_recv.at[near * CORES + me.core],
                device_id=me.chip(near, core, -1),
                device_id_type=MESH,
            )
        )
    other_core = pl.ds(SPREAD * UNIT, 2 * UNIT)
    shipped.append(
        pltpu.make_async_remote_copy(
            src_ref=res_ref.at[other_core],
            dst_ref=ret.at[other_core],
            send_sem=ship_send.at[SPREAD],
            recv_sem=ship_recv.at[SPREAD],
            device_id=me.sibling(),
            device_id_type=MESH,
        )
    )
    for copy in shipped:
        copy.start()

    def arrived(unit, ref):
        return pltpu.make_async_remote_copy(
            src_ref=ref, dst_ref=ref, send_sem=ship_recv.at[unit], recv_sem=ship_recv.at[unit],
            device_id=me.sibling(), device_id_type=MESH,
        ).wait_recv()

    for unit in range(SPREAD):
        arrived(unit, ret.at[pl.ds(unit * UNIT, UNIT)])
    arrived(SPREAD, ret.at[other_core])
    keep.wait()

    def gather(j, carry):
        send[j] = ret[jnp.maximum(meta_ref[3, j], 0)]
        return carry

    lax.fori_loop(0, count, gather, 0, unroll=4)

    def to_dom(off):
        other = lax.rem(me.dom + off, doms)
        return pltpu.make_async_remote_copy(
            src_ref=send.at[pl.ds(CAP_DOM * other, CAP_DOM)],
            dst_ref=back.at[pl.ds(CAP_DOM * me.dom, CAP_DOM)],
            send_sem=dom_send.at[off],
            recv_sem=dom_recv.at[off],
            device_id=(other, me.bin),
            device_id_type=MESH,
        )

    finish = exchange(doms, to_dom)
    for k in range(CAP_DOM):
        back[CAP_DOM * me.dom + k] = send[CAP_DOM * me.dom + k]
    finish()
    for b in range(blocks):
        picked[b] = back[meta_ref[4, b]]

    def to_bin(off):
        other = lax.rem(me.bin + off, bins)
        return pltpu.make_async_remote_copy(
            src_ref=picked.at[pl.ds(other * per, per)],
            dst_ref=final.at[pl.ds(me.bin * per, per)],
            send_sem=bin_send.at[off],
            recv_sem=bin_recv.at[off],
            device_id=(me.dom, other),
            device_id_type=MESH,
        )

    finish = exchange(bins, to_bin)
    for i in range(per):
        final[me.bin * per + i] = picked[me.bin * per + i]
    finish()
    bin_of = [bin_ref[b] for b in range(blocks)]
    place = [x * per + r for x, r in zip(bin_of, ranks(bin_of))]
    for b in range(blocks):
        out_ref[:, pl.ds(b * LANES, LANES)] = final[place[b]].reshape(VARS, LANES)
    for copy in shipped:
        copy.wait_send()


def local(points, candidates, block_dom, block_bin, block_slot, donor_nodes, donor_flow):
    bins, doms = lax.axis_size("bin"), lax.axis_size("dom")
    blocks = block_dom.shape[0]
    cells = donor_nodes.shape[1]
    held_blocks = cells // LANES
    count = doms * CAP_DOM
    places = GUEST * UNIT + count
    units = places // UNIT
    vmem = pl.BlockSpec(memory_space=pltpu.VMEM)
    smem = pl.BlockSpec(memory_space=pltpu.SMEM)
    hbm = pl.BlockSpec(memory_space=pl.ANY)
    dma = pltpu.SemaphoreType.DMA
    routes = [dma((bins,)), dma((bins,)), dma((doms,)), dma((doms,))]
    pairs = [dma((SPREAD + 1,)), dma((SPREAD + 1,))]
    node_map = jnp.asarray(monomial_map(3, NODE_ROWS), jnp.bfloat16)
    flow_map = jnp.asarray(monomial_map(VARS, FLOW_ROWS), jnp.bfloat16)

    work, meta, ext, own = pl.pallas_call(
        functools.partial(request_kernel, bins, doms, blocks, cells),
        out_shape=(
            jax.ShapeDtypeStruct((units, 4, UNIT, LANES), F32),
            jax.ShapeDtypeStruct((8, LANES), I32),
            jax.ShapeDtypeStruct((held_blocks, ROWS, LANES), F32),
            jax.ShapeDtypeStruct((held_blocks, ROWS, LANES), F32),
        ),
        in_specs=[smem, smem, smem, vmem, vmem, vmem, vmem, hbm, hbm],
        out_specs=(vmem, vmem, hbm, hbm),
        scratch_shapes=[
            pltpu.VMEM((blocks, 8, LANES), F32),
            pltpu.VMEM((blocks, 8, LANES), F32),
            pltpu.VMEM((blocks, 8, LANES), F32),
            pltpu.VMEM((doms, 8, LANES), F32),
            pltpu.VMEM((doms * 8, LANES), F32),
            pltpu.VMEM((GUEST, 4, UNIT, LANES), F32),
            pltpu.VMEM((81, cells), F32),
            pltpu.VMEM((135, cells), F32),
            pltpu.VMEM((held_blocks, ROWS, LANES), F32),
            dma((2, 4)), dma((2,)), *routes, *pairs, *pairs,
        ],
        compiler_params=pltpu.CompilerParams(collective_id=0, has_side_effects=True),
        name="request",
    )(
        block_bin, block_dom, block_slot, points, candidates, node_map, flow_map,
        donor_nodes, donor_flow,
    )

    result = pl.pallas_call(
        functools.partial(blend_kernel, GUEST * UNIT, places),
        out_shape=jax.ShapeDtypeStruct((places, VARS, 1, LANES), F32),
        in_specs=[smem, vmem, hbm, hbm],
        out_specs=vmem,
        scratch_shapes=[
            pltpu.VMEM((81, 16, LANES), F32),
            pltpu.VMEM((2, ROWS, LANES), F32),
            pltpu.SMEM((places,), I32),
            dma((2,)),
        ],
        name="blend",
    )(meta, work, ext, own)

    return pl.pallas_call(
        functools.partial(reply_kernel, bins, doms, blocks),
        out_shape=jax.ShapeDtypeStruct((VARS, points.shape[1]), F32),
        in_specs=[smem, smem, vmem],
        out_specs=vmem,
        scratch_shapes=[
            pltpu.VMEM((places, VARS, 1, LANES), F32),
            pltpu.VMEM((count, VARS, 1, LANES), F32),
            pltpu.VMEM((count, VARS, 1, LANES), F32),
            pltpu.VMEM((blocks, VARS, 1, LANES), F32),
            pltpu.VMEM((blocks, VARS, 1, LANES), F32),
            dma, *routes, *pairs,
        ],
        compiler_params=pltpu.CompilerParams(collective_id=1, has_side_effects=True),
        name="reply",
    )(block_bin, meta, result)


def solution(mesh):
    split = P(None, ("dom", "bin"))
    table = P(("dom", "bin"))
    return jax.shard_map(
        local,
        mesh=mesh,
        in_specs=(split, split, table, table, table, split, split),
        out_specs=split,
        check_vma=False,
    )
```

time: 167 us -> 110 us (0.66)
  Pallas kernels: 166 us -> 109 us
    pallas_call x1, Pallas kernels: 120 us -> 59.1 us  [local(): pl.pallas_call(functools.partial(reply_kernel, bins, doms, blocks), out_s...]
    pallas_call x2, Pallas kernels: 46 us -> 49.6 us  [the longest x1 41.4 us: local(): pl.pallas_call(functools.partial(request_kernel, bins, doms, blocks, cell...]
where the time goes in v2:
time: 110 us
  Pallas kernels  109 us (99%)
  local copies, waits for them, and re-layouts  1.47 us (1%)
    pallas_call x1, Pallas kernels, local(): pl.pallas_call(functools.partial(reply_kernel, bins, doms, blocks), out_s...  59.1 us
    pallas_call x1, Pallas kernels, local(): pl.pallas_call(functools.partial(request_kernel, bins, doms, blocks, cell...  41.4 us
    pallas_call x1, Pallas kernels, local(): pl.pallas_call(functools.partial(blend_kernel, GUEST * UNIT, places), out...  8.25 us

profile of v2, /device:TPU:1, one launch (start us, length us, event | category | flops | bytes accessed | tf_op | source)
XLA Modules:
  0.0 110.2 jit_solution(16310754094652376312)
XLA Ops:
  0.0 41.4 %request.1 = (f32[22,4,16,128]{3,2,1,0:T(8,128)}, s32[8,128]{1,0:T(8,128)}, f32[32,224,128]{2,1,0:T(8,128)}, f32[32,224,128]{2,1,0:T(8,128)}) custom-call(s32[16]{0:T(128)} %bin_ref.3, s32[16]{0:T(128)} %dom_ref.1, s32[16]{0:T(128)} %slot_ref.1, f32[3,2048]{1,0:T(4,128)} %pts_ref.1, s32[16,2048]{1,0:T(8,128)} %cand_ref.1, ...), custom_call_target="tpu_custom_call" | custom-call | tf_op jit(solution)/shard_map/request/pallas_call | solution.py:633
  41.4 8.3 %blend.1.res_ref = f32[352,5,1,128]{3,2,1,0:T(1,128)} custom-call(s32[8,128]{1,0:T(8,128)} %get-tuple-element.9.meta_ref, f32[22,4,16,128]{3,2,1,0:T(8,128)} %get-tuple-element.10.work_ref, f32[32,224,128]{2,1,0:T(8,128)} %get-tuple-element.11.ext_ref, f32[32,224,128]{2,1,0:T(8,128)} %get-tuple-element.12.own_ref), custom_call_target="tpu_custom_call" | custom-call | tf_op jit(solution)/shard_map/blend/pallas_call | solution.py:662
  49.6 59.1 %reply.1 = f32[5,2048]{1,0:T(8,128)} custom-call(s32[16]{0:T(128)} %bin_ref.3, s32[8,128]{1,0:T(8,128)} %get-tuple-element.9.meta_ref, f32[352,5,1,128]{3,2,1,0:T(1,128)} %blend.1.res_ref), custom_call_target="tpu_custom_call" | custom-call | tf_op jit(solution)/shard_map/reply/pallas_call | solution.py:676
  108.7 1.5 %copy.11 = f32[5,2048]{1,0:T(8,128)} copy(f32[5,2048]{1,0:T(8,128)} %reply.1) | data formatting | bytes 81920
